TPU v7x, 32 devices: a whole 2x2x4 slice. The times are simulated.
32 devices in a mesh: src: 16 (over z, x, core), tgt: 2 (over y).
Axes of the slice: x: 2, y: 2, z: 4, core: 2. Of those that a mesh axis runs over, the one named last changes fastest.
Arguments:
- source_embed: bfloat16 [128, 65536], P(None, 'src'), may hold values from -1 to 1
- target_embed: bfloat16 [128, 1024], P(None, 'tgt'), may hold values from -1 to 1
- source_expr: bfloat16 [128, 65536], P(None, 'src'), may hold values from -0.5390625 to 0.5390625
- target_expr: bfloat16 [128, 1024], P(None, 'tgt'), may hold values from -0.5390625 to 0.5390625
- current_plan: bfloat16 [65536, 1024], P('src', 'tgt'), as said below
- source_mass: float32 [65536], P('src'), may hold values from 0.25 to 4
- target_mass: float32 [1024], P('tgt'), may hold values from 0.25 to 4
- source_potential: float32 [65536], P('src'), may hold values from -16 to 16
- target_genes: bfloat16 [1024, 256], P('tgt'), may hold values from -6 to 6
Outputs:
- imputed: bfloat16 [65536, 256], P(('src', 'tgt'))
Inputs may be any that keep to these rules, and one draw needn't show every extreme that they name: Every entry of current_plan is positive.
All inputs are finite; a program needn't handle non-finite values.
Results may differ from a plain program's by a relative error of at most 0.014.
Values may be sent and summed in bfloat16 or wider, within the bound.
A program may use at most 64 MiB of HBM per device.

v0:
```python
import jax
import jax.numpy as jnp
from jax import lax
from jax.sharding import PartitionSpec as P

ITERS = 2
epsilon = 0.05
geometry_weight = 4.0


def joined(value, axis, join):
    pieces = jax.tree.map(lambda part: lax.all_gather(part, axis), value)
    head = jax.tree.map(lambda part: part[0], pieces)
    tail = jax.tree.map(lambda part: part[1:], pieces)
    so_far, _ = lax.scan(lambda so_far, piece: (join(so_far, piece), None), head, tail)
    return so_far


def factors(embed):
    widened = embed.astype(jnp.float32)
    squares = jnp.sum(widened * widened, axis=0)
    unit_row = jnp.ones_like(squares)
    left_factor = jnp.concatenate([squares[None, :], unit_row[None, :], -2.0 * widened], axis=0)
    right_factor = jnp.concatenate([unit_row[None, :], squares[None, :], widened], axis=0)
    return (left_factor, right_factor)


def combine_pair(earlier, later):
    maximum = jnp.maximum(earlier[0], later[0])
    return (
        maximum,
        earlier[1] * jnp.exp(earlier[0] - maximum) + later[1] * jnp.exp(later[0] - maximum),
    )


def column_logsum(scores):
    local_max = jnp.max(scores, axis=0)
    local_sum = jnp.sum(jnp.exp(scores - local_max[None, :]), axis=0)
    maximum, totals = joined((local_max, local_sum), "src", combine_pair)
    return maximum + jnp.log(totals)


def row_logsum(scores):
    local_max = jnp.max(scores, axis=1)
    local_sum = jnp.sum(jnp.exp(scores - local_max[:, None]), axis=1)
    maximum, totals = joined((local_max, local_sum), "tgt", combine_pair)
    return maximum + jnp.log(totals)


def shards(
    source_embed,
    target_embed,
    source_expr,
    target_expr,
    current_plan,
    source_mass,
    target_mass,
    source_potential,
    target_genes,
):
    highest = lax.Precision.HIGHEST
    spot_rows = source_embed.shape[1]
    spot_cols = target_embed.shape[1]
    total_pairs = float(spot_rows * lax.axis_size("src") * spot_cols * lax.axis_size("tgt"))
    left_src, right_src = factors(source_embed)
    left_tgt, right_tgt = factors(target_embed)
    projected = jnp.dot(
        current_plan.astype(jnp.float32),
        right_tgt.T,
        precision=highest,
        preferred_element_type=jnp.float32,
    )
    partial_core = jnp.dot(
        right_src, projected, precision=highest, preferred_element_type=jnp.float32
    )
    core_matrix = lax.psum(partial_core, ("src", "tgt")) / total_pairs
    geometry_right = jnp.dot(
        core_matrix, left_tgt, precision=highest, preferred_element_type=jnp.float32
    )
    geometry = lax.dot_general(
        left_src,
        geometry_right,
        (((0,), (0,)), ((), ())),
        precision=highest,
        preferred_element_type=jnp.float32,
    )
    feature = lax.dot_general(
        source_expr, target_expr, (((0,), (0,)), ((), ())), preferred_element_type=jnp.float32
    )
    cost_tile = -2.0 * (feature + geometry_weight * geometry)
    log_src = jnp.log(source_mass)
    log_tgt = jnp.log(target_mass)
    potential_src = source_potential
    potential_tgt = jnp.zeros((spot_cols,), jnp.float32)
    for iteration in range(ITERS):
        potential_tgt = epsilon * log_tgt - epsilon * column_logsum(
            (potential_src[:, None] - cost_tile) / epsilon
        )
        potential_src = epsilon * log_src - epsilon * row_logsum(
            (potential_tgt[None, :] - cost_tile) / epsilon
        )
    weights = jnp.exp(
        (potential_src[:, None] + potential_tgt[None, :] - cost_tile) / epsilon
    ).astype(jnp.bfloat16)
    row_share = spot_rows // lax.axis_size("tgt")
    row_offset = lax.axis_index("tgt") * row_share
    mass_rows = lax.dynamic_slice_in_dim(source_mass, row_offset, row_share)
    numerator = lax.psum_scatter(
        jnp.dot(weights, target_genes, preferred_element_type=jnp.float32).astype(jnp.bfloat16),
        "tgt",
        scatter_dimension=0,
        tiled=True,
    ).astype(jnp.float32)
    return (numerator / mass_rows[:, None]).astype(jnp.bfloat16)


def solution(mesh):
    return jax.shard_map(
        shards,
        mesh=mesh,
        in_specs=(
            P(None, "src"),
            P(None, "tgt"),
            P(None, "src"),
            P(None, "tgt"),
            P("src", "tgt"),
            P("src"),
            P("tgt"),
            P("src"),
            P("tgt", None),
        ),
        out_specs=P(("src", "tgt"), None),
        check_vma=False,
    )
```

profile of v0, /device:TPU:0, one launch (start us, length us, event | category | flops | bytes accessed | tf_op | source)
XLA Modules:
  0.0 319.4 jit_solution(5949856165096476949)
XLA Ops:
  6.5 0.0 copy-start
  6.5 0.0 all-reduce.2.cloned.1.call-start
  6.5 1.1 multiply_reduce_fusion.1
  7.7 1.2 convert_element_type.20
  8.9 1.6 broadcast_multiply_fusion
  10.4 1.4 convert_element_type.19
  11.9 0.0 copy-done.3
  11.9 4.3 %fusion.18 = f32[130,4096]{1,0:T(8,128)S(1)} fusion(bf16[4096,512]{1,0:T(8,128)(2,1)S(1)} %copy-done.3, f32[128,512]{1,0:T(8,128)S(1)} %convert_element_type.20, f32[1,512]{1,0:T(1,128)S(1)} %bitcast.56, f32[1,512]{1,0:T(1,128)S(1)} %broadcast.34), kind=kOutput, calls=%fused_computation.38 | convolution fusion | flops 3271690240 | bytes 6590464 | tf_op jit(solution)/shard_map/dot_general | solution.py:67
  16.2 2.8 fusion.12
  19.0 0.0 all-reduce.2.cloned.1.call-update
  19.0 0.2 reduce-scatter.2.cloned.1.call-start
  19.3 0.0 copy-done
  19.3 5.4 %fusion.50 = f32[4096,512]{1,0:T(8,128)} fusion(bf16[128,4096]{1,0:T(8,128)(2,1)S(1)} %copy-done, bf16[128,512]{1,0:T(8,128)(2,1)} %param.16), kind=kOutput, calls=%fused_computation.86 | convolution fusion | flops 536870912 | bytes 9568256 | tf_op jit(solution)/shard_map/dot_general | solution.py:87
  24.7 117.4 %all-reduce.2.cloned.1.call-done = f32[130,130]{1,0:T(8,128)} async-done(((f32[130,130]{1,0:T(8,128)}), f32[130,130]{1,0:T(8,128)}) %all-reduce.2.cloned.1.call-update) | async-done | bytes 67616 | tf_op jit(solution)/shard_map/psum | solution.py:76
  142.1 1.3 fusion.24
  143.4 0.0 copy-done.5
  143.4 11.4 %fusion = (f32[512]{0:T(512)S(1)}, f32[4096,512]{1,0:T(8,128)S(1)}) fusion(f32[4096]{0:T(1024)S(1)} %copy-done.5, f32[4096,512]{1,0:T(8,128)} %fusion.50, f32[130,512]{1,0:T(8,128)S(1)} %fusion.24, f32[128,4096]{1,0:T(8,128)S(1)} %get-tuple-element.123, f32[1,4096]{1,0:T(1,128)S(1)} %broadcast.33, f32[1,4096]{1,0:T(1,128)S(1)} %bitcast.47), kind=kOutput, calls=%fused_computation.16 | convolution fusion | flops 3285204480 | bytes 19191808 | tf_op jit(solution)/shard_map/dot_general | solution.py:80
  154.8 0.0 copy-start.1
  154.8 0.0 copy-start.6
  154.8 3.2 %copy-done.1 = f32[4096,512]{1,0:T(8,128)} copy-done((f32[4096,512]{1,0:T(8,128)}, f32[4096,512]{1,0:T(8,128)S(1)}, u32[]{:S(2)}) %copy-start.1) | copy-done | bytes 8388632
  158.0 1.8 exponential_reduce_fusion.3
  159.8 22.9 %all-gather.9 = f32[16,1,512]{2,1,0:T(1,128)S(1)} all-gather(f32[1,1,512]{2,1,0:T(1,128)S(1)} %bitcast.61), channel_id=3, replica_groups=mesh['src'=16,'tgt'=2] {'src'}, dimensions={0}, use_global_device_ids=true | all-gather | bytes 34816 | tf_op jit(solution)/shard_map/all_gather | solution.py:12
  182.7 17.5 %all-gather.8 = f32[16,1,512]{2,1,0:T(1,128)S(1)} all-gather(f32[1,1,512]{2,1,0:T(1,128)S(1)} %bitcast.58), channel_id=2, replica_groups=mesh['src'=16,'tgt'=2] {'src'}, dimensions={0}, use_global_device_ids=true | all-gather | bytes 34816 | tf_op jit(solution)/shard_map/all_gather | solution.py:12
  200.2 0.8 while.4
  201.0 0.0 copy-start.2
  201.0 0.0 copy-done.6
  201.0 0.0 copy-start.4
  201.1 4.4 %fusion.1 = f32[4096]{0:T(1024)S(1)} fusion(f32[4096,512]{1,0:T(8,128)} %copy-done.1, f32[512]{0:T(512)S(1)} %multiply_subtract_fusion.1), kind=kLoop, calls=%fused_computation.17 | loop fusion | flops 6287360 | bytes 8407040 | tf_op jit(solution)/shard_map/reduce_max | solution.py:44
  205.5 1.3 copy-done.2
  206.8 2.2 exponential_reduce_fusion.2
  209.0 4.4 %all-gather.2 = f32[8192]{0:T(1024)S(1)} all-gather(f32[4096]{0:T(1024)S(1)} %fusion.1), channel_id=4, replica_groups=mesh['src'=16,'tgt'=2] {'tgt'}, dimensions={0}, use_global_device_ids=true | all-gather | bytes 49152 | tf_op jit(solution)/shard_map/all_gather | solution.py:12
  213.4 4.4 %all-gather.3 = f32[8192]{0:T(1024)S(1)} all-gather(f32[4096]{0:T(1024)S(1)} %exponential_reduce_fusion.2), channel_id=5, replica_groups=mesh['src'=16,'tgt'=2] {'tgt'}, dimensions={0}, use_global_device_ids=true | all-gather | bytes 49152 | tf_op jit(solution)/shard_map/all_gather | solution.py:12
  217.8 1.0 fusion.2
  218.8 1.8 exponential_reduce_fusion.1
  220.6 18.9 %all-gather.11 = f32[16,1,512]{2,1,0:T(1,128)S(1)} all-gather(f32[1,1,512]{2,1,0:T(1,128)S(1)} %bitcast.60), channel_id=7, replica_groups=mesh['src'=16,'tgt'=2] {'src'}, dimensions={0}, use_global_device_ids=true | all-gather | bytes 34816 | tf_op jit(solution)/shard_map/all_gather | solution.py:12
  239.5 17.7 %all-gather.10 = f32[16,1,512]{2,1,0:T(1,128)S(1)} all-gather(f32[1,1,512]{2,1,0:T(1,128)S(1)} %bitcast.59), channel_id=6, replica_groups=mesh['src'=16,'tgt'=2] {'src'}, dimensions={0}, use_global_device_ids=true | all-gather | bytes 34816 | tf_op jit(solution)/shard_map/all_gather | solution.py:12
  257.2 0.8 while.5
  258.1 0.0 slice-start
  258.1 0.0 copy-start.7
  258.1 4.4 %fusion.3 = f32[4096]{0:T(1024)S(1)} fusion(f32[4096,512]{1,0:T(8,128)} %copy-done.1, f32[512]{0:T(512)S(1)} %multiply_subtract_fusion), kind=kLoop, calls=%fused_computation.19 | loop fusion | flops 6287360 | bytes 8407040 | tf_op jit(solution)/shard_map/reduce_max | solution.py:44
  262.5 0.0 slice-start.1
  262.5 5.1 %exponential_reduce_fusion = f32[4096]{0:T(1024)S(1)} fusion(f32[4096,512]{1,0:T(8,128)} %copy-done.1, f32[4096]{0:T(1024)S(1)} %fusion.3, f32[512]{0:T(512)S(1)} %multiply_subtract_fusion), kind=kLoop, calls=%fused_computation.7 | loop fusion | flops 8384512 | bytes 8423424 | tf_op jit(solution)/shard_map/reduce_sum | solution.py:45
  267.6 4.4 %all-gather.6 = f32[8192]{0:T(1024)S(1)} all-gather(f32[4096]{0:T(1024)S(1)} %fusion.3), channel_id=8, replica_groups=mesh['src'=16,'tgt'=2] {'tgt'}, dimensions={0}, use_global_device_ids=true | all-gather | bytes 49152 | tf_op jit(solution)/shard_map/all_gather | solution.py:12
  272.0 4.4 %all-gather.7 = f32[8192]{0:T(1024)S(1)} all-gather(f32[4096]{0:T(1024)S(1)} %exponential_reduce_fusion), channel_id=9, replica_groups=mesh['src'=16,'tgt'=2] {'tgt'}, dimensions={0}, use_global_device_ids=true | all-gather | bytes 49152 | tf_op jit(solution)/shard_map/all_gather | solution.py:12
  276.5 3.2 %convolution_convert_fusion = bf16[4096,256]{1,0:T(8,128)(2,1)} fusion(bf16[512,256]{1,0:T(8,128)(2,1)S(1)} %copy-done.7, f32[4096,512]{1,0:T(8,128)S(1)} %bitcast.41, f32[4096]{0:T(1024)S(1)} %fusion.36, f32[512]{0:T(512)S(1)} %multiply_subtract_fusion), kind=kOutput, calls=%fused_computation.20 | convolution fusion | flops 1083179008 | bytes 10766336 | tf_op jit(solution)/shard_map/dot_general | solution.py:109
  279.7 0.0 reduce-scatter.2.cloned.1.call-update
  279.8 30.3 %reduce-scatter.2.cloned.1.call-done = bf16[2048,256]{1,0:T(8,128)(2,1)} async-done(((bf16[4096,256]{1,0:T(8,128)(2,1)}), bf16[2048,256]{1,0:T(8,128)(2,1)}) %reduce-scatter.2.cloned.1.call-update) | async-done | bytes 1048592 | tf_op jit(solution)/shard_map/reduce_scatter | solution.py:108
  310.1 2.5 divide_convert_fusion
  (86 shorter events, 1.1 us)
Async XLA Ops:
  6.5 12.7 %copy-start = (bf16[128,4096]{1,0:T(8,128)(2,1)S(1)}, bf16[128,4096]{1,0:T(8,128)(2,1)}, u32[]{:S(2)}) copy-start(bf16[128,4096]{1,0:T(8,128)(2,1)} %param.15) | copy-start | bytes 3145732
  6.5 135.5 %all-reduce.2.cloned.1.call-start = ((), (), s32[]{:S(2)}) async-start(), calls=%async_computation.1 | async-start | bytes 278528 | tf_op jit(solution)/shard_map/psum | solution.py:76
  6.5 5.4 %copy-start.3 = (bf16[4096,512]{1,0:T(8,128)(2,1)S(1)}, bf16[4096,512]{1,0:T(8,128)(2,1)}, u32[]{:S(2)}) copy-start(bf16[4096,512]{1,0:T(8,128)(2,1)} %param.17) | copy-start | bytes 12582916
  19.0 124.4 %copy-start.5 = (f32[4096]{0:T(1024)S(1)}, f32[4096]{0:T(1024)}, u32[]{:S(2)}) copy-start(f32[4096]{0:T(1024)} %param.20) | copy-start | bytes 49156
  19.0 291.0 %reduce-scatter.2.cloned.1.call-start = ((), (), s32[]{:S(2)}) async-start(), calls=%async_computation.2 | async-start | bytes 3145728 | tf_op jit(solution)/shard_map/reduce_scatter | solution.py:108
  154.8 3.2 %copy-start.1 = (f32[4096,512]{1,0:T(8,128)}, f32[4096,512]{1,0:T(8,128)S(1)}, u32[]{:S(2)}) copy-start(f32[4096,512]{1,0:T(8,128)S(1)} %get-tuple-element.128) | copy-start | bytes 25165828
  154.8 46.2 %copy-start.6 = (f32[512]{0:T(512)S(1)}, f32[512]{0:T(512)}, u32[]{:S(2)}) copy-start(f32[512]{0:T(512)} %param.19) | copy-start | bytes 6148
  201.0 5.8 %copy-start.2 = (f32[4096,512]{1,0:T(8,128)S(1)}, f32[4096,512]{1,0:T(8,128)}, u32[]{:S(2)}) copy-start(f32[4096,512]{1,0:T(8,128)} %copy-done.1) | copy-start | bytes 25165828
  201.0 16.8 %copy-start.4 = (f32[4096]{0:T(1024)S(1)}, f32[4096]{0:T(1024)}, u32[]{:S(2)}) copy-start(f32[4096]{0:T(1024)} %param.18) | copy-start | bytes 49156
  258.1 18.4 %slice-start = ((s8[8388608]{0:T(1024)(128)(4,1)}), s8[4194304]{0:T(1024)(128)(4,1)S(1)}, s32[]{:S(2)}) async-start(s8[8388608]{0:T(1024)(128)(4,1)} %bitcast.40), calls=%async_computation.3 | async-start | bytes 8388608
  258.1 18.4 %copy-start.7 = (bf16[512,256]{1,0:T(8,128)(2,1)S(1)}, bf16[512,256]{1,0:T(8,128)(2,1)}, u32[]{:S(2)}) copy-start(bf16[512,256]{1,0:T(8,128)(2,1)} %param.21) | copy-start | bytes 786436
  262.5 14.0 %slice-start.1 = ((s8[8388608]{0:T(1024)(128)(4,1)}), s8[4194304]{0:T(1024)(128)(4,1)S(1)}, s32[]{:S(2)}) async-start(s8[8388608]{0:T(1024)(128)(4,1)} %bitcast.40), calls=%async_computation.4 | async-start | bytes 8388608
Sparse Core Ops, SparseCore 0:
  19.1 122.8 all-reduce.1
  279.9 30.1 reduce-scatter.1
where the time goes:
time: 320 us; the launch traced here: 319 us
  waiting for transfers between devices  148 us (46%)
  blocking collectives  94.5 us (30%)
  other arithmetic  29.3 us (9%)
  matrix products  28.4 us (9%)
  between operations  13.7 us (4%)
  local copies, waits for them, and re-layouts  4.93 us (2%)
    psum x1, waiting for transfers between devices, shards(): core_matrix = lax.psum(partial_core, ('src', 'tgt')) / total_pairs  117 us
    all_gather x8, blocking collectives, joined(): pieces = jax.tree.map(lambda part: lax.all_gather(part, axis), value)  94.5 us
    reduce_scatter x1, waiting for transfers between devices, shards(): lax.psum_scatter(jnp.dot(weights, target_genes, preferred_element_type=jn...  30.3 us
    dot_general x1, matrix products, shards(): lax.dot_general(left_src, geometry_right, (((0,), (0,)), ((), ())), preci...  11.4 us
    reduce_max x2, other arithmetic, row_logsum(): local_max = jnp.max(scores, axis=1)  8.87 us
    reduce_sum x2, other arithmetic, row_logsum(): local_sum = jnp.sum(jnp.exp(scores - local_max[:, None]), axis=1)  7.28 us
  transfers between devices with their start and end apart: 2, of which 2 were waited for; matrix products, arithmetic and copies ran while one was open for 2% of the time, Pallas kernels for 0%

commit v1 on v0

--- a/solution.py
+++ b/solution.py
@@ -73,7 +73,15 @@
     partial_core = jnp.dot(
         right_src, projected, precision=highest, preferred_element_type=jnp.float32
     )
-    core_matrix = lax.psum(partial_core, ("src", "tgt")) / total_pairs
+
+    def spread_run(body):
+        named_axis = "src"
+        mesh_dim = "tgt"
+        for dev_i in (mesh_dim, named_axis):
+            body = lax.psum(body, dev_i)
+        return body
+
+    core_matrix = spread_run(partial_core) / total_pairs
     geometry_right = jnp.dot(
         core_matrix, left_tgt, precision=highest, preferred_element_type=jnp.float32
     )

time: 320 us -> 311 us (0.972)
  waiting for transfers between devices: 148 us -> 140 us
    psum x1 -> x2, waiting for transfers between devices: 117 us -> 110 us  [spread_run(): body = lax.psum(body, dev_i)]
  transfers between devices with their start and end apart: 2 -> 3, of which waited for: 2 -> 3; matrix products, arithmetic and copies ran while one was open for 2% -> 2% of each run, Pallas kernels for 0% -> 0%
where the time goes in v1:
time: 311 us; the launch traced here: 310 us
  waiting for transfers between devices  140 us (45%)
  blocking collectives  93.1 us (30%)
  other arithmetic  29.3 us (9%)
  matrix products  28.4 us (9%)
  between operations  13.4 us (4%)
  local copies, waits for them, and re-layouts  4.93 us (2%)
    psum x2, waiting for transfers between devices, spread_run(): body = lax.psum(body, dev_i)  110 us
    all_gather x8, blocking collectives, joined(): pieces = jax.tree.map(lambda part: lax.all_gather(part, axis), value)  93.1 us
    reduce_scatter x1, waiting for transfers between devices, shards(): lax.psum_scatter(jnp.dot(weights, target_genes, preferred_element_type=jn...  30.3 us
    dot_general x1, matrix products, shards(): lax.dot_general(left_src, geometry_right, (((0,), (0,)), ((), ())), preci...  11.4 us
    reduce_max x2, other arithmetic, row_logsum(): local_max = jnp.max(scores, axis=1)  8.87 us
    reduce_sum x2, other arithmetic, row_logsum(): local_sum = jnp.sum(jnp.exp(scores - local_max[:, None]), axis=1)  7.28 us
  transfers between devices with their start and end apart: 3, of which 3 were waited for; matrix products, arithmetic and copies ran while one was open for 2% of the time, Pallas kernels for 0%

profile of v1, /device:TPU:0, one launch (start us, length us, event | category | flops | bytes accessed | tf_op | source)
XLA Modules:
  0.0 310.4 jit_solution(6774343998640118646)
XLA Ops:
  6.5 0.0 copy-start
  6.5 0.0 all-reduce.3.cloned.1.call-start
  6.5 1.1 multiply_reduce_fusion.1
  7.7 1.2 convert_element_type.20
  8.9 1.6 broadcast_multiply_fusion
  10.4 1.4 convert_element_type.19
  11.9 0.0 copy-done.3
  11.9 4.3 %fusion.18 = f32[130,4096]{1,0:T(8,128)S(1)} fusion(bf16[4096,512]{1,0:T(8,128)(2,1)S(1)} %copy-done.3, f32[128,512]{1,0:T(8,128)S(1)} %convert_element_type.20, f32[1,512]{1,0:T(1,128)S(1)} %bitcast.56, f32[1,512]{1,0:T(1,128)S(1)} %broadcast.34), kind=kOutput, calls=%fused_computation.38 | convolution fusion | flops 3271690240 | bytes 6590464 | tf_op jit(solution)/shard_map/dot_general | solution.py:67
  16.2 2.8 fusion.12
  19.0 0.0 all-reduce.3.cloned.1.call-update
  19.0 0.0 all-reduce.5.cloned.1.call-start
  19.1 24.4 %all-reduce.3.cloned.1.call-done = f32[130,130]{1,0:T(8,128)} async-done(((f32[130,130]{1,0:T(8,128)}), f32[130,130]{1,0:T(8,128)}) %all-reduce.3.cloned.1.call-update) | async-done | bytes 67616 | tf_op jit(solution)/shard_map/psum | solution.py:81
  43.4 0.0 all-reduce.5.cloned.1.call-update
  43.5 0.2 reduce-scatter.2.cloned.1.call-start
  43.7 0.0 copy-done
  43.7 5.4 %fusion.50 = f32[4096,512]{1,0:T(8,128)} fusion(bf16[128,4096]{1,0:T(8,128)(2,1)S(1)} %copy-done, bf16[128,512]{1,0:T(8,128)(2,1)} %param.16), kind=kOutput, calls=%fused_computation.86 | convolution fusion | flops 536870912 | bytes 9568256 | tf_op jit(solution)/shard_map/dot_general | solution.py:95
  49.1 85.6 %all-reduce.5.cloned.1.call-done = f32[130,130]{1,0:T(8,128)} async-done(((f32[130,130]{1,0:T(8,128)}), f32[130,130]{1,0:T(8,128)}) %all-reduce.5.cloned.1.call-update) | async-done | bytes 67616 | tf_op jit(solution)/shard_map/psum | solution.py:81
  134.7 1.3 fusion.24
  136.0 0.0 copy-done.5
  136.1 11.4 %fusion = (f32[512]{0:T(512)S(1)}, f32[4096,512]{1,0:T(8,128)S(1)}) fusion(f32[4096]{0:T(1024)S(1)} %copy-done.5, f32[4096,512]{1,0:T(8,128)} %fusion.50, f32[130,512]{1,0:T(8,128)S(1)} %fusion.24, f32[128,4096]{1,0:T(8,128)S(1)} %get-tuple-element.123, f32[1,4096]{1,0:T(1,128)S(1)} %broadcast.33, f32[1,4096]{1,0:T(1,128)S(1)} %bitcast.47), kind=kOutput, calls=%fused_computation.16 | convolution fusion | flops 3285204480 | bytes 19191808 | tf_op jit(solution)/shard_map/dot_general | solution.py:88
  147.4 0.0 copy-start.6
  147.5 3.2 %copy-done.1 = f32[4096,512]{1,0:T(8,128)} copy-done((f32[4096,512]{1,0:T(8,128)}, f32[4096,512]{1,0:T(8,128)S(1)}, u32[]{:S(2)}) %copy-start.1) | copy-done | bytes 8388632
  150.7 1.8 exponential_reduce_fusion.3
  152.5 21.4 %all-gather.9 = f32[16,1,512]{2,1,0:T(1,128)S(1)} all-gather(f32[1,1,512]{2,1,0:T(1,128)S(1)} %bitcast.61), channel_id=3, replica_groups=mesh['src'=16,'tgt'=2] {'src'}, dimensions={0}, use_global_device_ids=true | all-gather | bytes 34816 | tf_op jit(solution)/shard_map/all_gather | solution.py:12
  173.9 17.5 %all-gather.8 = f32[16,1,512]{2,1,0:T(1,128)S(1)} all-gather(f32[1,1,512]{2,1,0:T(1,128)S(1)} %bitcast.58), channel_id=2, replica_groups=mesh['src'=16,'tgt'=2] {'src'}, dimensions={0}, use_global_device_ids=true | all-gather | bytes 34816 | tf_op jit(solution)/shard_map/all_gather | solution.py:12
  191.4 0.8 while.4
  192.2 0.0 copy-start.4
  192.3 4.4 %fusion.1 = f32[4096]{0:T(1024)S(1)} fusion(f32[4096,512]{1,0:T(8,128)} %copy-done.1, f32[512]{0:T(512)S(1)} %multiply_subtract_fusion.1), kind=kLoop, calls=%fused_computation.17 | loop fusion | flops 6287360 | bytes 8407040 | tf_op jit(solution)/shard_map/reduce_max | solution.py:44
  196.7 1.3 copy-done.2
  198.0 2.2 exponential_reduce_fusion.2
  200.2 4.4 %all-gather.2 = f32[8192]{0:T(1024)S(1)} all-gather(f32[4096]{0:T(1024)S(1)} %fusion.1), channel_id=4, replica_groups=mesh['src'=16,'tgt'=2] {'tgt'}, dimensions={0}, use_global_device_ids=true | all-gather | bytes 49152 | tf_op jit(solution)/shard_map/all_gather | solution.py:12
  204.6 4.4 %all-gather.3 = f32[8192]{0:T(1024)S(1)} all-gather(f32[4096]{0:T(1024)S(1)} %exponential_reduce_fusion.2), channel_id=5, replica_groups=mesh['src'=16,'tgt'=2] {'tgt'}, dimensions={0}, use_global_device_ids=true | all-gather | bytes 49152 | tf_op jit(solution)/shard_map/all_gather | solution.py:12
  209.0 1.0 fusion.2
  210.0 1.8 exponential_reduce_fusion.1
  211.8 18.9 %all-gather.11 = f32[16,1,512]{2,1,0:T(1,128)S(1)} all-gather(f32[1,1,512]{2,1,0:T(1,128)S(1)} %bitcast.60), channel_id=7, replica_groups=mesh['src'=16,'tgt'=2] {'src'}, dimensions={0}, use_global_device_ids=true | all-gather | bytes 34816 | tf_op jit(solution)/shard_map/all_gather | solution.py:12
  230.7 17.7 %all-gather.10 = f32[16,1,512]{2,1,0:T(1,128)S(1)} all-gather(f32[1,1,512]{2,1,0:T(1,128)S(1)} %bitcast.59), channel_id=6, replica_groups=mesh['src'=16,'tgt'=2] {'src'}, dimensions={0}, use_global_device_ids=true | all-gather | bytes 34816 | tf_op jit(solution)/shard_map/all_gather | solution.py:12
  248.4 0.8 while.5
  249.2 0.0 slice-start
  249.3 0.0 copy-start.7
  249.3 4.4 %fusion.3 = f32[4096]{0:T(1024)S(1)} fusion(f32[4096,512]{1,0:T(8,128)} %copy-done.1, f32[512]{0:T(512)S(1)} %multiply_subtract_fusion), kind=kLoop, calls=%fused_computation.19 | loop fusion | flops 6287360 | bytes 8407040 | tf_op jit(solution)/shard_map/reduce_max | solution.py:44
  253.7 0.0 slice-start.1
  253.7 5.1 %exponential_reduce_fusion = f32[4096]{0:T(1024)S(1)} fusion(f32[4096,512]{1,0:T(8,128)} %copy-done.1, f32[4096]{0:T(1024)S(1)} %fusion.3, f32[512]{0:T(512)S(1)} %multiply_subtract_fusion), kind=kLoop, calls=%fused_computation.7 | loop fusion | flops 8384512 | bytes 8423424 | tf_op jit(solution)/shard_map/reduce_sum | solution.py:45
  258.8 4.4 %all-gather.6 = f32[8192]{0:T(1024)S(1)} all-gather(f32[4096]{0:T(1024)S(1)} %fusion.3), channel_id=8, replica_groups=mesh['src'=16,'tgt'=2] {'tgt'}, dimensions={0}, use_global_device_ids=true | all-gather | bytes 49152 | tf_op jit(solution)/shard_map/all_gather | solution.py:12
  263.2 4.4 %all-gather.7 = f32[8192]{0:T(1024)S(1)} all-gather(f32[4096]{0:T(1024)S(1)} %exponential_reduce_fusion), channel_id=9, replica_groups=mesh['src'=16,'tgt'=2] {'tgt'}, dimensions={0}, use_global_device_ids=true | all-gather | bytes 49152 | tf_op jit(solution)/shard_map/all_gather | solution.py:12
  267.7 3.2 %convolution_convert_fusion = bf16[4096,256]{1,0:T(8,128)(2,1)} fusion(bf16[512,256]{1,0:T(8,128)(2,1)S(1)} %copy-done.7, f32[4096,512]{1,0:T(8,128)S(1)} %bitcast.41, f32[4096]{0:T(1024)S(1)} %fusion.36, f32[512]{0:T(512)S(1)} %multiply_subtract_fusion), kind=kOutput, calls=%fused_computation.20 | convolution fusion | flops 1083179008 | bytes 10766336 | tf_op jit(solution)/shard_map/dot_general | solution.py:117
  270.9 0.0 reduce-scatter.2.cloned.1.call-update
  271.0 30.3 %reduce-scatter.2.cloned.1.call-done = bf16[2048,256]{1,0:T(8,128)(2,1)} async-done(((bf16[4096,256]{1,0:T(8,128)(2,1)}), bf16[2048,256]{1,0:T(8,128)(2,1)}) %reduce-scatter.2.cloned.1.call-update) | async-done | bytes 1048592 | tf_op jit(solution)/shard_map/reduce_scatter | solution.py:116
  301.3 2.5 divide_convert_fusion
  (89 shorter events, 1.1 us)
Async XLA Ops:
  6.5 37.2 %copy-start = (bf16[128,4096]{1,0:T(8,128)(2,1)S(1)}, bf16[128,4096]{1,0:T(8,128)(2,1)}, u32[]{:S(2)}) copy-start(bf16[128,4096]{1,0:T(8,128)(2,1)} %param.15) | copy-start | bytes 3145732
  6.5 36.9 %all-reduce.3.cloned.1.call-start = ((), (), s32[]{:S(2)}) async-start(), calls=%async_computation.1 | async-start | bytes 278528 | tf_op jit(solution)/shard_map/psum | solution.py:81
  6.5 5.4 %copy-start.3 = (bf16[4096,512]{1,0:T(8,128)(2,1)S(1)}, bf16[4096,512]{1,0:T(8,128)(2,1)}, u32[]{:S(2)}) copy-start(bf16[4096,512]{1,0:T(8,128)(2,1)} %param.17) | copy-start | bytes 12582916
  19.0 117.0 %copy-start.5 = (f32[4096]{0:T(1024)S(1)}, f32[4096]{0:T(1024)}, u32[]{:S(2)}) copy-start(f32[4096]{0:T(1024)} %param.20) | copy-start | bytes 49156
  19.0 115.7 %all-reduce.5.cloned.1.call-start = ((), (), s32[]{:S(2)}) async-start(), calls=%async_computation.2 | async-start | bytes 278528 | tf_op jit(solution)/shard_map/psum | solution.py:81
  43.5 257.8 %reduce-scatter.2.cloned.1.call-start = ((), (), s32[]{:S(2)}) async-start(), calls=%async_computation.3 | async-start | bytes 3145728 | tf_op jit(solution)/shard_map/reduce_scatter | solution.py:116
  147.4 3.2 %copy-start.1 = (f32[4096,512]{1,0:T(8,128)}, f32[4096,512]{1,0:T(8,128)S(1)}, u32[]{:S(2)}) copy-start(f32[4096,512]{1,0:T(8,128)S(1)} %get-tuple-element.128) | copy-start | bytes 25165828
  147.4 44.8 %copy-start.6 = (f32[512]{0:T(512)S(1)}, f32[512]{0:T(512)}, u32[]{:S(2)}) copy-start(f32[512]{0:T(512)} %param.19) | copy-start | bytes 6148
  192.2 5.8 %copy-start.2 = (f32[4096,512]{1,0:T(8,128)S(1)}, f32[4096,512]{1,0:T(8,128)}, u32[]{:S(2)}) copy-start(f32[4096,512]{1,0:T(8,128)} %copy-done.1) | copy-start | bytes 25165828
  192.2 16.8 %copy-start.4 = (f32[4096]{0:T(1024)S(1)}, f32[4096]{0:T(1024)}, u32[]{:S(2)}) copy-start(f32[4096]{0:T(1024)} %param.18) | copy-start | bytes 49156
  249.2 18.4 %slice-start = ((s8[8388608]{0:T(1024)(128)(4,1)}), s8[4194304]{0:T(1024)(128)(4,1)S(1)}, s32[]{:S(2)}) async-start(s8[8388608]{0:T(1024)(128)(4,1)} %bitcast.40), calls=%async_computation.4 | async-start | bytes 8388608
  249.3 18.4 %copy-start.7 = (bf16[512,256]{1,0:T(8,128)(2,1)S(1)}, bf16[512,256]{1,0:T(8,128)(2,1)}, u32[]{:S(2)}) copy-start(bf16[512,256]{1,0:T(8,128)(2,1)} %param.21) | copy-start | bytes 786436
  253.7 14.0 %slice-start.1 = ((s8[8388608]{0:T(1024)(128)(4,1)}), s8[4194304]{0:T(1024)(128)(4,1)S(1)}, s32[]{:S(2)}) async-start(s8[8388608]{0:T(1024)(128)(4,1)} %bitcast.40), calls=%async_computation.5 | async-start | bytes 8388608
Sparse Core Ops, SparseCore 0:
  19.1 24.2 all-reduce.2
  46.9 87.7 all-reduce.4
  271.1 30.1 reduce-scatter.1
